TPU v7x, 128 devices: a whole 4x4x4 slice. The times are simulated.
128 devices in a mesh: dp: 16 (over z, x), pipe: 8 (over y, core).
Axes of the slice: x: 4, y: 4, z: 4, core: 2. Of those that a mesh axis runs over, the one named last changes fastest.
Arguments:
- tokens: bfloat16 [128, 64, 3072], P('dp'), may hold values from -40 to 40
- segments: int32 [128, 64], P('dp'), may hold values from 0 to 5, never falling along the last dimension, each value on 1 to 24 neighbouring positions
- keep_mask: int32 [128, 64], P('dp'), may hold values 0 or 1
- norm_gain: float32 [8, 3072], P('pipe'), may hold values from 0.5 to 2
- norm_bias: float32 [8, 3072], P('pipe'), may hold values from -3 to 3
- w_qkv: bfloat16 [8, 3072, 4608], P('pipe', 'dp'), may hold values from -0.109375 to 0.109375
- w_out: bfloat16 [8, 1536, 3072], P('pipe', 'dp'), may hold values from -0.15625 to 0.15625
Outputs:
- layer_outputs: bfloat16 [8, 128, 64, 3072], P('pipe', 'dp')
Inputs may be any that keep to these rules, and one draw needn't show every extreme that they name: `segments`: image numbers never fall along a sequence; every image spans 1 to 24 patches and one spans exactly 24.
All inputs are finite; a program needn't handle non-finite values. No bound on the sum of `keep_mask` on one device may be relied on, other than what follows from the above.
Results may differ from a plain program's by a relative error of at most 0.013.
Values may be sent and summed in bfloat16 or wider, within the bound.
No kernel may reach another device: no remote copies, remote signals or barrier semaphores. Data moves between devices by JAX's collectives and lax.ppermute only.
A program may use at most 128 MiB of HBM per device.

v0:
```python
import math

import jax
import jax.numpy as jnp
from jax import lax
from jax.sharding import PartitionSpec as P

D = 3072
HEADS = 24
HD = 64
GROUPS = 32
IMGS = 6
INNER = 1536


norm_eps = 1e-05


def passed_along(value, axis, steps):
    count = lax.axis_size(axis)
    first, last = (max(0, -steps), min(count, count - steps))
    return lax.ppermute(value, axis, [(source, source + steps) for source in range(first, last)])


def group_normed(stream, seg_row, keep_row, gain, bias_row):
    length = stream.shape[0]
    group_width = D // GROUPS
    values = stream.astype(jnp.float32).reshape(length, GROUPS, group_width)
    member = (
        (seg_row[:, None] == jnp.arange(IMGS, dtype=jnp.int32)[None, :]) & (keep_row[:, None] > 0)
    ).astype(jnp.float32)
    counted = jnp.maximum(jnp.sum(member, axis=0) * group_width, 1.0)
    img_sum = jnp.dot(member.T, jnp.sum(values, axis=2), precision=lax.Precision.HIGHEST)
    img_mean = img_sum / counted[:, None]
    tok_mean = jnp.dot(member, img_mean, precision=lax.Precision.HIGHEST)
    centred = values - tok_mean[:, :, None]
    img_var = (
        jnp.dot(member.T, jnp.sum(centred * centred, axis=2), precision=lax.Precision.HIGHEST)
        / counted[:, None]
    )
    tok_var = jnp.dot(member, img_var, precision=lax.Precision.HIGHEST)
    normed = (centred * lax.rsqrt(tok_var + norm_eps)[:, :, None]).reshape(length, D)
    normed = (normed * gain[None, :] + bias_row[None, :]) * keep_row[:, None].astype(jnp.float32)
    return normed.astype(jnp.bfloat16)


def attend(stream, seg_row, keep_row, gain, bias_row, qkv_weight):
    length = stream.shape[0]
    normed = group_normed(stream, seg_row, keep_row, gain, bias_row)
    projected = jnp.dot(normed, qkv_weight, preferred_element_type=jnp.float32)
    query_rows = projected[:, :INNER].reshape(length, HEADS, HD)
    key_rows = projected[:, INNER : 2 * INNER].reshape(length, HEADS, HD)
    value_rows = projected[:, 2 * INNER :].reshape(length, HEADS, HD).astype(jnp.bfloat16)
    query_rows = (
        query_rows * lax.rsqrt(jnp.mean(query_rows * query_rows, axis=2, keepdims=True) + 1e-06)
    ).astype(jnp.bfloat16)
    key_rows = (
        key_rows * lax.rsqrt(jnp.mean(key_rows * key_rows, axis=2, keepdims=True) + 1e-06)
    ).astype(jnp.bfloat16)
    scores = jnp.einsum(
        "qhd,khd->hqk", query_rows, key_rows, preferred_element_type=jnp.float32
    ) / math.sqrt(HD)
    keep_float = keep_row.astype(jnp.float32)
    allowed = (
        (seg_row[:, None] == seg_row[None, :]).astype(jnp.float32)
        * keep_float[:, None]
        * keep_float[None, :]
    )
    expo = jnp.exp(scores) * allowed[None, :, :]
    denominator = jnp.sum(expo, axis=2) + (1.0 - keep_float)[None, :]
    probs = (expo / denominator[:, :, None]).astype(jnp.bfloat16)
    attended = jnp.einsum("hqk,khd->qhd", probs, value_rows, preferred_element_type=jnp.float32)
    return attended.reshape(length, INNER).astype(jnp.bfloat16)


def finish(stream, attended, out_weight):
    branch = jnp.dot(attended, out_weight, preferred_element_type=jnp.float32)
    return (stream.astype(jnp.float32) + branch).astype(jnp.bfloat16)


def advance(stream):
    return passed_along(stream, "pipe", 1)


def local(tokens, segments, keep_mask, norm_gain, norm_bias, w_qkv, w_out):
    section_no = lax.axis_index("pipe")
    sections = lax.axis_size("pipe")
    micro = tokens.shape[0]
    gain = norm_gain[0]
    bias_row = norm_bias[0]
    saved = jnp.zeros((1,) + tokens.shape, jnp.bfloat16)

    def store(saved, result, micro_idx):
        is_live = (micro_idx >= 0) & (micro_idx < micro)
        clipped = jnp.clip(micro_idx, 0, micro - 1)
        kept = jnp.where(is_live, result, saved[0, clipped])
        return lax.dynamic_update_slice(saved, kept[None, None], (0, clipped, 0, 0))

    incoming = jnp.zeros(tokens.shape[1:], jnp.bfloat16)
    qkv_all, out_all = (
        lax.all_gather(w_qkv, "dp", axis=1, tiled=True),
        lax.all_gather(w_out, "dp", axis=1, tiled=True),
    )
    state = (incoming, saved)
    qkv_full = qkv_all[0]
    out_full = out_all[0]

    def tick(tick_no, running):
        incoming, saved_now = running
        micro_idx = tick_no - section_no
        is_live = (micro_idx >= 0) & (micro_idx < micro)
        clipped = jnp.clip(micro_idx, 0, micro - 1)
        section_input = jnp.where(section_no == 0, tokens[clipped], incoming)
        seg_row = segments[clipped]
        keep_row = keep_mask[clipped]

        def compute(stream):
            return finish(
                stream, attend(stream, seg_row, keep_row, gain, bias_row, qkv_full), out_full
            )

        def pass_on(stream):
            return stream

        result = lax.cond(is_live, compute, pass_on, section_input)
        saved_now = store(saved_now, result, micro_idx)
        return (advance(result), saved_now)

    final_state = lax.fori_loop(0, micro + sections - 1, tick, state)
    return final_state[1]


def solution(mesh):
    placed = (
        P("dp", None, None),
        P("dp", None),
        P("dp", None),
        P("pipe", None),
        P("pipe", None),
        P("pipe", "dp", None),
        P("pipe", "dp", None),
    )
    return jax.shard_map(
        local, mesh=mesh, in_specs=placed, out_specs=P("pipe", "dp", None, None), check_vma=False
    )
```

profile of v0, /device:TPU:25, one launch (start us, length us, event | category | flops | bytes accessed | tf_op | source)
XLA Modules:
  0.0 810.2 jit_solution(16699117233308174468)
XLA Ops:
  8.0 79.1 %all-gather.5.cloned.1.call-done = bf16[1,1536,3072]{2,1,0:T(8,128)(2,1)} async-done(((bf16[1,96,3072]{2,1,0:T(8,128)(2,1)}), bf16[1,1536,3072]{2,1,0:T(8,128)(2,1)}) %all-gather.5.cloned.1.call-update) | async-done | bytes 9437200 | tf_op jit(solution)/shard_map/all_gather | solution.py:102
  87.1 172.1 %all-gather.3.cloned.1.call-done = bf16[1,3072,4608]{2,1,0:T(8,128)(2,1)} async-done(((bf16[1,192,4608]{2,1,0:T(8,128)(2,1)}), bf16[1,3072,4608]{2,1,0:T(8,128)(2,1)}) %all-gather.3.cloned.1.call-update) | async-done | bytes 28311568 | tf_op jit(solution)/shard_map/all_gather | solution.py:101
  261.3 542.0 %while.16 = (s32[]{:T(128)}, bf16[64,3072]{1,0:T(8,128)(2,1)S(1)}, bf16[1,8,64,3072]{3,2,1,0:T(8,128)(2,1)}, s32[]{:T(128)}, pred[]{:T(512)}, /*index=5*/bf16[8,...) while((s32[]{:T(128)}, bf16[64,3072]{1,0:T(8,128)(2,1)S(1)}, ...), condition=%wide.region_9.10_spmd, body=%wide.region_0.9_spmd.sunk | while | flops 2446215168 | bytes 66486384 | solution.py:129
  270.6 5.9 collective-permute-done
  280.7 5.9 collective-permute-done
  290.9 5.9 collective-permute-done
  301.1 5.9 collective-permute-done
  311.2 5.9 collective-permute-done
  321.4 181.2 %collective-permute-done = bf16[64,3072]{1,0:T(8,128)(2,1)S(1)} collective-permute-done((bf16[64,3072]{1,0:T(8,128)(2,1)S(1)}, bf16[64,3072]{1,0:T(8,128)(2,1)S(1)}, u32[]{:S(2)}, u32[]{:S(2)}) %collective-permute-start) | collective-permute-done | bytes 393248 | tf_op jit(solution)/shard_map/while/body/eval_jaxpr/ppermute | solution.py:22
  503.7 28.1 %conditional.2 = (bf16[64,3072]{1,0:T(8,128)(2,1)S(1)}) conditional(s32[]{:T(128)} %convert_element_type.94, bf16[64,3072]{1,0:T(8,128)(2,1)S(1)} %bitcast_select_fusion.3, (bf16[64,3072]{1,0:T(8,128)(2,1)S(1)}, s32[8,64]{1,0:T(8,128)}, s32[]{:T(128)}, s32[8,64]{1,0:T(8,128)}, f32[1,3072]{1,0:T(1,128)S(1)}, /*index=5*/f32[1,3072]{1,0:T(1,128)S(1)}, ...), branch_computations={%region_1.1_spmd, %region_2.8_spmd} | conditional | flops 2445821952 | bytes 61766956 | solution.py:125
  510.1 11.7 %fusion.4 = f32[64,4608]{1,0:T(8,128)S(1)} fusion(bf16[3072,4608]{1,0:T(8,128)(2,1)} %get-tuple-element.298, f32[64,3072]{1,0:T(8,128)S(1)} %mul.104, f32[64,3072]{1,0:T(8,128)S(1)} %sub.25, f32[64]{0:T(128)S(1)} %get-tuple-element.340, f32[3072]{0:T(1024)S(1)} %bitcast.42, f32[3072]{0:T(1024)S(1)} %bitcast.41, bf16[64,3072]{1,0:T(8,128)(2,1)S(1)} %get-tuple-element.292), kind=kOutput, calls=%fused_computation.17 | convolution fusion | flops 1813315584 | bytes 31482112 | tf_op jit(solution)/shard_map/while/body/eval_jaxpr/cond/branch_1_fun/dot_general | solution.py:50
  535.0 5.9 collective-permute-done
  541.9 28.1 %conditional.2 = (bf16[64,3072]{1,0:T(8,128)(2,1)S(1)}) conditional(s32[]{:T(128)} %convert_element_type.94, bf16[64,3072]{1,0:T(8,128)(2,1)S(1)} %bitcast_select_fusion.3, (bf16[64,3072]{1,0:T(8,128)(2,1)S(1)}, s32[8,64]{1,0:T(8,128)}, s32[]{:T(128)}, s32[8,64]{1,0:T(8,128)}, f32[1,3072]{1,0:T(1,128)S(1)}, /*index=5*/f32[1,3072]{1,0:T(1,128)S(1)}, ...), branch_computations={%region_1.1_spmd, %region_2.8_spmd} | conditional | flops 2445821952 | bytes 61766956 | solution.py:125
  548.4 11.7 %fusion.4 = f32[64,4608]{1,0:T(8,128)S(1)} fusion(bf16[3072,4608]{1,0:T(8,128)(2,1)} %get-tuple-element.298, f32[64,3072]{1,0:T(8,128)S(1)} %mul.104, f32[64,3072]{1,0:T(8,128)S(1)} %sub.25, f32[64]{0:T(128)S(1)} %get-tuple-element.340, f32[3072]{0:T(1024)S(1)} %bitcast.42, f32[3072]{0:T(1024)S(1)} %bitcast.41, bf16[64,3072]{1,0:T(8,128)(2,1)S(1)} %get-tuple-element.292), kind=kOutput, calls=%fused_computation.17 | convolution fusion | flops 1813315584 | bytes 31482112 | tf_op jit(solution)/shard_map/while/body/eval_jaxpr/cond/branch_1_fun/dot_general | solution.py:50
  573.2 5.9 collective-permute-done
  580.2 28.1 %conditional.2 = (bf16[64,3072]{1,0:T(8,128)(2,1)S(1)}) conditional(s32[]{:T(128)} %convert_element_type.94, bf16[64,3072]{1,0:T(8,128)(2,1)S(1)} %bitcast_select_fusion.3, (bf16[64,3072]{1,0:T(8,128)(2,1)S(1)}, s32[8,64]{1,0:T(8,128)}, s32[]{:T(128)}, s32[8,64]{1,0:T(8,128)}, f32[1,3072]{1,0:T(1,128)S(1)}, /*index=5*/f32[1,3072]{1,0:T(1,128)S(1)}, ...), branch_computations={%region_1.1_spmd, %region_2.8_spmd} | conditional | flops 2445821952 | bytes 61766956 | solution.py:125
  586.6 11.7 %fusion.4 = f32[64,4608]{1,0:T(8,128)S(1)} fusion(bf16[3072,4608]{1,0:T(8,128)(2,1)} %get-tuple-element.298, f32[64,3072]{1,0:T(8,128)S(1)} %mul.104, f32[64,3072]{1,0:T(8,128)S(1)} %sub.25, f32[64]{0:T(128)S(1)} %get-tuple-element.340, f32[3072]{0:T(1024)S(1)} %bitcast.42, f32[3072]{0:T(1024)S(1)} %bitcast.41, bf16[64,3072]{1,0:T(8,128)(2,1)S(1)} %get-tuple-element.292), kind=kOutput, calls=%fused_computation.17 | convolution fusion | flops 1813315584 | bytes 31482112 | tf_op jit(solution)/shard_map/while/body/eval_jaxpr/cond/branch_1_fun/dot_general | solution.py:50
  611.5 5.9 collective-permute-done
  618.5 28.1 %conditional.2 = (bf16[64,3072]{1,0:T(8,128)(2,1)S(1)}) conditional(s32[]{:T(128)} %convert_element_type.94, bf16[64,3072]{1,0:T(8,128)(2,1)S(1)} %bitcast_select_fusion.3, (bf16[64,3072]{1,0:T(8,128)(2,1)S(1)}, s32[8,64]{1,0:T(8,128)}, s32[]{:T(128)}, s32[8,64]{1,0:T(8,128)}, f32[1,3072]{1,0:T(1,128)S(1)}, /*index=5*/f32[1,3072]{1,0:T(1,128)S(1)}, ...), branch_computations={%region_1.1_spmd, %region_2.8_spmd} | conditional | flops 2445821952 | bytes 61766956 | solution.py:125
  624.9 11.7 %fusion.4 = f32[64,4608]{1,0:T(8,128)S(1)} fusion(bf16[3072,4608]{1,0:T(8,128)(2,1)} %get-tuple-element.298, f32[64,3072]{1,0:T(8,128)S(1)} %mul.104, f32[64,3072]{1,0:T(8,128)S(1)} %sub.25, f32[64]{0:T(128)S(1)} %get-tuple-element.340, f32[3072]{0:T(1024)S(1)} %bitcast.42, f32[3072]{0:T(1024)S(1)} %bitcast.41, bf16[64,3072]{1,0:T(8,128)(2,1)S(1)} %get-tuple-element.292), kind=kOutput, calls=%fused_computation.17 | convolution fusion | flops 1813315584 | bytes 31482112 | tf_op jit(solution)/shard_map/while/body/eval_jaxpr/cond/branch_1_fun/dot_general | solution.py:50
  649.8 5.9 collective-permute-done
  656.8 28.1 %conditional.2 = (bf16[64,3072]{1,0:T(8,128)(2,1)S(1)}) conditional(s32[]{:T(128)} %convert_element_type.94, bf16[64,3072]{1,0:T(8,128)(2,1)S(1)} %bitcast_select_fusion.3, (bf16[64,3072]{1,0:T(8,128)(2,1)S(1)}, s32[8,64]{1,0:T(8,128)}, s32[]{:T(128)}, s32[8,64]{1,0:T(8,128)}, f32[1,3072]{1,0:T(1,128)S(1)}, /*index=5*/f32[1,3072]{1,0:T(1,128)S(1)}, ...), branch_computations={%region_1.1_spmd, %region_2.8_spmd} | conditional | flops 2445821952 | bytes 61766956 | solution.py:125
  663.2 11.7 %fusion.4 = f32[64,4608]{1,0:T(8,128)S(1)} fusion(bf16[3072,4608]{1,0:T(8,128)(2,1)} %get-tuple-element.298, f32[64,3072]{1,0:T(8,128)S(1)} %mul.104, f32[64,3072]{1,0:T(8,128)S(1)} %sub.25, f32[64]{0:T(128)S(1)} %get-tuple-element.340, f32[3072]{0:T(1024)S(1)} %bitcast.42, f32[3072]{0:T(1024)S(1)} %bitcast.41, bf16[64,3072]{1,0:T(8,128)(2,1)S(1)} %get-tuple-element.292), kind=kOutput, calls=%fused_computation.17 | convolution fusion | flops 1813315584 | bytes 31482112 | tf_op jit(solution)/shard_map/while/body/eval_jaxpr/cond/branch_1_fun/dot_general | solution.py:50
  688.1 5.9 collective-permute-done
  695.0 28.1 %conditional.2 = (bf16[64,3072]{1,0:T(8,128)(2,1)S(1)}) conditional(s32[]{:T(128)} %convert_element_type.94, bf16[64,3072]{1,0:T(8,128)(2,1)S(1)} %bitcast_select_fusion.3, (bf16[64,3072]{1,0:T(8,128)(2,1)S(1)}, s32[8,64]{1,0:T(8,128)}, s32[]{:T(128)}, s32[8,64]{1,0:T(8,128)}, f32[1,3072]{1,0:T(1,128)S(1)}, /*index=5*/f32[1,3072]{1,0:T(1,128)S(1)}, ...), branch_computations={%region_1.1_spmd, %region_2.8_spmd} | conditional | flops 2445821952 | bytes 61766956 | solution.py:125
  701.5 11.7 %fusion.4 = f32[64,4608]{1,0:T(8,128)S(1)} fusion(bf16[3072,4608]{1,0:T(8,128)(2,1)} %get-tuple-element.298, f32[64,3072]{1,0:T(8,128)S(1)} %mul.104, f32[64,3072]{1,0:T(8,128)S(1)} %sub.25, f32[64]{0:T(128)S(1)} %get-tuple-element.340, f32[3072]{0:T(1024)S(1)} %bitcast.42, f32[3072]{0:T(1024)S(1)} %bitcast.41, bf16[64,3072]{1,0:T(8,128)(2,1)S(1)} %get-tuple-element.292), kind=kOutput, calls=%fused_computation.17 | convolution fusion | flops 1813315584 | bytes 31482112 | tf_op jit(solution)/shard_map/while/body/eval_jaxpr/cond/branch_1_fun/dot_general | solution.py:50
  726.3 5.9 collective-permute-done
  733.3 28.1 %conditional.2 = (bf16[64,3072]{1,0:T(8,128)(2,1)S(1)}) conditional(s32[]{:T(128)} %convert_element_type.94, bf16[64,3072]{1,0:T(8,128)(2,1)S(1)} %bitcast_select_fusion.3, (bf16[64,3072]{1,0:T(8,128)(2,1)S(1)}, s32[8,64]{1,0:T(8,128)}, s32[]{:T(128)}, s32[8,64]{1,0:T(8,128)}, f32[1,3072]{1,0:T(1,128)S(1)}, /*index=5*/f32[1,3072]{1,0:T(1,128)S(1)}, ...), branch_computations={%region_1.1_spmd, %region_2.8_spmd} | conditional | flops 2445821952 | bytes 61766956 | solution.py:125
  739.7 11.7 %fusion.4 = f32[64,4608]{1,0:T(8,128)S(1)} fusion(bf16[3072,4608]{1,0:T(8,128)(2,1)} %get-tuple-element.298, f32[64,3072]{1,0:T(8,128)S(1)} %mul.104, f32[64,3072]{1,0:T(8,128)S(1)} %sub.25, f32[64]{0:T(128)S(1)} %get-tuple-element.340, f32[3072]{0:T(1024)S(1)} %bitcast.42, f32[3072]{0:T(1024)S(1)} %bitcast.41, bf16[64,3072]{1,0:T(8,128)(2,1)S(1)} %get-tuple-element.292), kind=kOutput, calls=%fused_computation.17 | convolution fusion | flops 1813315584 | bytes 31482112 | tf_op jit(solution)/shard_map/while/body/eval_jaxpr/cond/branch_1_fun/dot_general | solution.py:50
  764.6 5.9 collective-permute-done
  771.6 28.1 %conditional.2 = (bf16[64,3072]{1,0:T(8,128)(2,1)S(1)}) conditional(s32[]{:T(128)} %convert_element_type.94, bf16[64,3072]{1,0:T(8,128)(2,1)S(1)} %bitcast_select_fusion.3, (bf16[64,3072]{1,0:T(8,128)(2,1)S(1)}, s32[8,64]{1,0:T(8,128)}, s32[]{:T(128)}, s32[8,64]{1,0:T(8,128)}, f32[1,3072]{1,0:T(1,128)S(1)}, /*index=5*/f32[1,3072]{1,0:T(1,128)S(1)}, ...), branch_computations={%region_1.1_spmd, %region_2.8_spmd} | conditional | flops 2445821952 | bytes 61766956 | solution.py:125
  778.0 11.7 %fusion.4 = f32[64,4608]{1,0:T(8,128)S(1)} fusion(bf16[3072,4608]{1,0:T(8,128)(2,1)} %get-tuple-element.298, f32[64,3072]{1,0:T(8,128)S(1)} %mul.104, f32[64,3072]{1,0:T(8,128)S(1)} %sub.25, f32[64]{0:T(128)S(1)} %get-tuple-element.340, f32[3072]{0:T(1024)S(1)} %bitcast.42, f32[3072]{0:T(1024)S(1)} %bitcast.41, bf16[64,3072]{1,0:T(8,128)(2,1)S(1)} %get-tuple-element.292), kind=kOutput, calls=%fused_computation.17 | convolution fusion | flops 1813315584 | bytes 31482112 | tf_op jit(solution)/shard_map/while/body/eval_jaxpr/cond/branch_1_fun/dot_general | solution.py:50
  (351 shorter events, 198.1 us)
Async XLA Ops:
  6.5 254.7 %copy-start.1 = (f32[1,3072]{1,0:T(1,128)S(1)}, f32[1,3072]{1,0:T(1,128)}, u32[]{:S(2)}) copy-start(f32[1,3072]{1,0:T(1,128)} %param.14) | copy-start | bytes 36868
  6.5 254.8 %copy-start.2 = (f32[1,3072]{1,0:T(1,128)S(1)}, f32[1,3072]{1,0:T(1,128)}, u32[]{:S(2)}) copy-start(f32[1,3072]{1,0:T(1,128)} %param.15) | copy-start | bytes 36868
  6.5 80.6 %all-gather.5.cloned.1.call-start = ((), (), s32[]{:S(2)}) async-start(), calls=%async_computation.1 | async-start | bytes 10027008 | tf_op jit(solution)/shard_map/all_gather | solution.py:102
  7.3 251.9 %all-gather.3.cloned.1.call-start = ((), (), s32[]{:S(2)}) async-start(), calls=%async_computation | async-start | bytes 30081024 | tf_op jit(solution)/shard_map/all_gather | solution.py:101
  262.4 4.0 collective-permute-start
  267.4 9.1 %collective-permute-start = (bf16[64,3072]{1,0:T(8,128)(2,1)S(1)}, bf16[64,3072]{1,0:T(8,128)(2,1)S(1)}, u32[]{:S(2)}, u32[]{:S(2)}) collective-permute-start(bf16[64,3072]{1,0:T(8,128)(2,1)S(1)} %get-tuple-element.468), channel_id=1, source_target_pairs={{0,1},{1,2},{2,3},{3,4},{4,5},{5,6},{6,7},{8,9},{9,10},{10,11},{11... | collective-permute-start | bytes 1179656 | tf_op jit(solution)/shard_map/while/body/eval_jaxpr/ppermute | solution.py:22
  277.6 9.1 %collective-permute-start = (bf16[64,3072]{1,0:T(8,128)(2,1)S(1)}, bf16[64,3072]{1,0:T(8,128)(2,1)S(1)}, u32[]{:S(2)}, u32[]{:S(2)}) collective-permute-start(bf16[64,3072]{1,0:T(8,128)(2,1)S(1)} %get-tuple-element.468), channel_id=1, source_target_pairs={{0,1},{1,2},{2,3},{3,4},{4,5},{5,6},{6,7},{8,9},{9,10},{10,11},{11... | collective-permute-start | bytes 1179656 | tf_op jit(solution)/shard_map/while/body/eval_jaxpr/ppermute | solution.py:22
  287.7 9.1 %collective-permute-start = (bf16[64,3072]{1,0:T(8,128)(2,1)S(1)}, bf16[64,3072]{1,0:T(8,128)(2,1)S(1)}, u32[]{:S(2)}, u32[]{:S(2)}) collective-permute-start(bf16[64,3072]{1,0:T(8,128)(2,1)S(1)} %get-tuple-element.468), channel_id=1, source_target_pairs={{0,1},{1,2},{2,3},{3,4},{4,5},{5,6},{6,7},{8,9},{9,10},{10,11},{11... | collective-permute-start | bytes 1179656 | tf_op jit(solution)/shard_map/while/body/eval_jaxpr/ppermute | solution.py:22
  297.9 9.1 %collective-permute-start = (bf16[64,3072]{1,0:T(8,128)(2,1)S(1)}, bf16[64,3072]{1,0:T(8,128)(2,1)S(1)}, u32[]{:S(2)}, u32[]{:S(2)}) collective-permute-start(bf16[64,3072]{1,0:T(8,128)(2,1)S(1)} %get-tuple-element.468), channel_id=1, source_target_pairs={{0,1},{1,2},{2,3},{3,4},{4,5},{5,6},{6,7},{8,9},{9,10},{10,11},{11... | collective-permute-start | bytes 1179656 | tf_op jit(solution)/shard_map/while/body/eval_jaxpr/ppermute | solution.py:22
  308.0 9.1 %collective-permute-start = (bf16[64,3072]{1,0:T(8,128)(2,1)S(1)}, bf16[64,3072]{1,0:T(8,128)(2,1)S(1)}, u32[]{:S(2)}, u32[]{:S(2)}) collective-permute-start(bf16[64,3072]{1,0:T(8,128)(2,1)S(1)} %get-tuple-element.468), channel_id=1, source_target_pairs={{0,1},{1,2},{2,3},{3,4},{4,5},{5,6},{6,7},{8,9},{9,10},{10,11},{11... | collective-permute-start | bytes 1179656 | tf_op jit(solution)/shard_map/while/body/eval_jaxpr/ppermute | solution.py:22
  318.2 184.4 %collective-permute-start = (bf16[64,3072]{1,0:T(8,128)(2,1)S(1)}, bf16[64,3072]{1,0:T(8,128)(2,1)S(1)}, u32[]{:S(2)}, u32[]{:S(2)}) collective-permute-start(bf16[64,3072]{1,0:T(8,128)(2,1)S(1)} %get-tuple-element.468), channel_id=1, source_target_pairs={{0,1},{1,2},{2,3},{3,4},{4,5},{5,6},{6,7},{8,9},{9,10},{10,11},{11... | collective-permute-start | bytes 1179656 | tf_op jit(solution)/shard_map/while/body/eval_jaxpr/ppermute | solution.py:22
  521.8 1.0 copy-start
  531.8 9.1 %collective-permute-start = (bf16[64,3072]{1,0:T(8,128)(2,1)S(1)}, bf16[64,3072]{1,0:T(8,128)(2,1)S(1)}, u32[]{:S(2)}, u32[]{:S(2)}) collective-permute-start(bf16[64,3072]{1,0:T(8,128)(2,1)S(1)} %get-tuple-element.468), channel_id=1, source_target_pairs={{0,1},{1,2},{2,3},{3,4},{4,5},{5,6},{6,7},{8,9},{9,10},{10,11},{11... | collective-permute-start | bytes 1179656 | tf_op jit(solution)/shard_map/while/body/eval_jaxpr/ppermute | solution.py:22
  560.1 1.0 copy-start
  570.1 9.1 %collective-permute-start = (bf16[64,3072]{1,0:T(8,128)(2,1)S(1)}, bf16[64,3072]{1,0:T(8,128)(2,1)S(1)}, u32[]{:S(2)}, u32[]{:S(2)}) collective-permute-start(bf16[64,3072]{1,0:T(8,128)(2,1)S(1)} %get-tuple-element.468), channel_id=1, source_target_pairs={{0,1},{1,2},{2,3},{3,4},{4,5},{5,6},{6,7},{8,9},{9,10},{10,11},{11... | collective-permute-start | bytes 1179656 | tf_op jit(solution)/shard_map/while/body/eval_jaxpr/ppermute | solution.py:22
  598.3 1.0 copy-start
  608.3 9.1 %collective-permute-start = (bf16[64,3072]{1,0:T(8,128)(2,1)S(1)}, bf16[64,3072]{1,0:T(8,128)(2,1)S(1)}, u32[]{:S(2)}, u32[]{:S(2)}) collective-permute-start(bf16[64,3072]{1,0:T(8,128)(2,1)S(1)} %get-tuple-element.468), channel_id=1, source_target_pairs={{0,1},{1,2},{2,3},{3,4},{4,5},{5,6},{6,7},{8,9},{9,10},{10,11},{11... | collective-permute-start | bytes 1179656 | tf_op jit(solution)/shard_map/while/body/eval_jaxpr/ppermute | solution.py:22
  636.6 1.0 copy-start
  646.6 9.1 %collective-permute-start = (bf16[64,3072]{1,0:T(8,128)(2,1)S(1)}, bf16[64,3072]{1,0:T(8,128)(2,1)S(1)}, u32[]{:S(2)}, u32[]{:S(2)}) collective-permute-start(bf16[64,3072]{1,0:T(8,128)(2,1)S(1)} %get-tuple-element.468), channel_id=1, source_target_pairs={{0,1},{1,2},{2,3},{3,4},{4,5},{5,6},{6,7},{8,9},{9,10},{10,11},{11... | collective-permute-start | bytes 1179656 | tf_op jit(solution)/shard_map/while/body/eval_jaxpr/ppermute | solution.py:22
  674.9 1.0 copy-start
  684.9 9.1 %collective-permute-start = (bf16[64,3072]{1,0:T(8,128)(2,1)S(1)}, bf16[64,3072]{1,0:T(8,128)(2,1)S(1)}, u32[]{:S(2)}, u32[]{:S(2)}) collective-permute-start(bf16[64,3072]{1,0:T(8,128)(2,1)S(1)} %get-tuple-element.468), channel_id=1, source_target_pairs={{0,1},{1,2},{2,3},{3,4},{4,5},{5,6},{6,7},{8,9},{9,10},{10,11},{11... | collective-permute-start | bytes 1179656 | tf_op jit(solution)/shard_map/while/body/eval_jaxpr/ppermute | solution.py:22
  713.1 1.0 copy-start
  723.2 9.1 %collective-permute-start = (bf16[64,3072]{1,0:T(8,128)(2,1)S(1)}, bf16[64,3072]{1,0:T(8,128)(2,1)S(1)}, u32[]{:S(2)}, u32[]{:S(2)}) collective-permute-start(bf16[64,3072]{1,0:T(8,128)(2,1)S(1)} %get-tuple-element.468), channel_id=1, source_target_pairs={{0,1},{1,2},{2,3},{3,4},{4,5},{5,6},{6,7},{8,9},{9,10},{10,11},{11... | collective-permute-start | bytes 1179656 | tf_op jit(solution)/shard_map/while/body/eval_jaxpr/ppermute | solution.py:22
  751.4 1.0 copy-start
  761.4 9.1 %collective-permute-start = (bf16[64,3072]{1,0:T(8,128)(2,1)S(1)}, bf16[64,3072]{1,0:T(8,128)(2,1)S(1)}, u32[]{:S(2)}, u32[]{:S(2)}) collective-permute-start(bf16[64,3072]{1,0:T(8,128)(2,1)S(1)} %get-tuple-element.468), channel_id=1, source_target_pairs={{0,1},{1,2},{2,3},{3,4},{4,5},{5,6},{6,7},{8,9},{9,10},{10,11},{11... | collective-permute-start | bytes 1179656 | tf_op jit(solution)/shard_map/while/body/eval_jaxpr/ppermute | solution.py:22
  789.7 1.0 copy-start
  799.7 3.6 collective-permute-start
Sparse Core Ops, SparseCore 0:
  9.5 77.6 all-gather.4
  89.3 169.8 all-gather.2
where the time goes:
time: 813 us; the launch traced here: 810 us
  waiting for transfers between devices  506 us (62%)
  matrix products  148 us (18%)
  local copies, waits for them, and re-layouts  63.6 us (8%)
  other arithmetic  57.7 us (7%)
  starting transfers between devices  19.4 us (2%)
  between operations  13.4 us (2%)
    ppermute x15, waiting for transfers between devices, passed_along(): lax.ppermute(value, axis, [(source, source + steps) for source in range(f...  254 us
    all_gather x1, waiting for transfers between devices, local(): lax.all_gather(w_qkv, 'dp', axis=1, tiled=True)  172 us
    dot_general x8, matrix products, attend(): projected = jnp.dot(normed, qkv_weight, preferred_element_type=jnp.float32)  93.4 us
    all_gather x1, waiting for transfers between devices, local(): lax.all_gather(w_out, 'dp', axis=1, tiled=True)  79.1 us
    dot_general x8, matrix products, finish(): branch = jnp.dot(attended, out_weight, preferred_element_type=jnp.float32)  44 us
    ppermute x15, starting transfers between devices, passed_along(): lax.ppermute(value, axis, [(source, source + steps) for source in range(f...  19.4 us
  transfers between devices with their start and end apart: 17, of which 17 were waited for; matrix products, arithmetic and copies ran while one was open for 3% of the time, Pallas kernels for 0%

commit v1 on v0

v1 whole, which is shorter than its diff:
```python
import math

import jax
import jax.numpy as jnp
from jax import lax
from jax.experimental import pallas as pl
from jax.experimental.pallas import tpu as pltpu
from jax.sharding import PartitionSpec as P

D = 3072
HEADS = 24
HD = 64
GROUPS = 32
IMGS = 6
INNER = 1536
WIDTH = D // GROUPS
LEN = 64
PER = 2
ROWS = PER * LEN
BLOCK = 256
BF = jnp.bfloat16
F32 = jnp.float32

norm_eps = 1e-05


def parts(value, count):
    found = []
    for at in range(count):
        piece = value.astype(BF)
        found.append(piece)
        if at + 1 < count:
            value = value - piece.astype(F32)
    return found


def dot(a, b):
    return jnp.dot(a, b, preferred_element_type=F32)


def dot_nt(a, b):
    return lax.dot_general(a, b, (((1,), (1,)), ((), ())), preferred_element_type=F32)


def group_normed(x, code_c, code_r, gain, bias):
    slots = PER * 8
    slot = lax.broadcasted_iota(jnp.int32, (ROWS, slots), 1)
    row = lax.broadcasted_iota(jnp.int32, (ROWS, slots), 0)
    member = ((code_c == slot % 8) & (row // LEN == slot // 8)).astype(F32)
    member_t = jnp.concatenate(
        [
            jnp.concatenate(
                [
                    (code_r[at] == lax.broadcasted_iota(jnp.int32, (8, LEN), 0)).astype(BF)
                    if at == seq
                    else jnp.zeros((8, LEN), BF)
                    for at in range(PER)
                ],
                axis=1,
            )
            for seq in range(PER)
        ],
        axis=0,
    )
    ch = lax.broadcasted_iota(jnp.int32, (D, GROUPS), 0)
    low = lax.broadcasted_iota(jnp.int32, (D, GROUPS), 1) * WIDTH
    to_group = ((ch >= low) & (ch < low + WIDTH)).astype(BF)
    ch = lax.broadcasted_iota(jnp.int32, (GROUPS * 3, D), 1)
    low = lax.broadcasted_iota(jnp.int32, (GROUPS * 3, D), 0) % GROUPS * WIDTH
    to_channel = ((ch >= low) & (ch < low + WIDTH)).astype(BF)
    counted = jnp.maximum(jnp.sum(member_t.astype(F32), axis=1, keepdims=True) * WIDTH, 1.0)
    member3 = jnp.concatenate([member] * 3, axis=1).astype(BF)

    def group_mean(per_image):
        sums = dot(jnp.concatenate(parts(per_image, 3), axis=0), to_group)
        return (sums[:slots] + sums[slots : 2 * slots] + sums[2 * slots :]) / counted

    def of_tokens(per_image):
        return dot(member3, jnp.concatenate(parts(per_image, 3), axis=0))

    def of_channels(per_group):
        return dot(jnp.concatenate(parts(per_group, 3), axis=1), to_channel)

    mean = group_mean(dot(member_t, x))
    centred = x.astype(F32) - of_channels(of_tokens(mean))
    square = parts(centred * centred, 2)
    var = group_mean(dot(member_t, square[0]) + dot(member_t, square[1]))
    inverse = lax.rsqrt(of_tokens(var) + norm_eps)
    kept = (code_c >= 0).astype(F32)
    return ((centred * of_channels(inverse) * gain + bias) * kept).astype(BF)


def tick_kernel(
    now_ref, at_ref, incoming_ref, tokens_ref, code_c_ref, code_r_ref, gain_ref, bias_ref, w_ref, saved_in_ref,
    out_ref, saved_ref, x_ref, normed_ref, attended_ref, y_ref, held_ref, sem, w_sem, out_sem,
):
    del saved_in_ref
    mine = now_ref[0] - at_ref[0]
    micros = tokens_ref.shape[0]
    micro = jnp.clip(mine, 0, micros - 1)

    def load(j):
        cols = pl.ds(j % 6 * BLOCK, BLOCK)
        rows = pl.ds(0, 576) if j < 6 else pl.ds(576, 192)
        return pltpu.make_async_copy(w_ref.at[:, rows, cols], held_ref.at[:, rows, cols], w_sem.at[j])

    def wq(part, j):
        return held_ref[:, part * 192 : (part + 1) * 192, j * BLOCK : (j + 1) * BLOCK].reshape(D, BLOCK)

    def wo(c):
        top = 576 + 96 * (c // 6)
        return held_ref[:, top : top + 96, c % 6 * BLOCK : (c % 6 + 1) * BLOCK].reshape(INNER, BLOCK)

    @pl.when((mine >= 0) & (mine < micros))
    def _():
        @pl.when(at_ref[0] == 0)
        def _():
            pltpu.make_async_copy(tokens_ref.at[micro], x_ref, sem.at[0]).start()

        @pl.when(at_ref[0] != 0)
        def _():
            pltpu.make_async_copy(incoming_ref, x_ref, sem.at[0]).start()

        for j in range(12):
            load(j).start()
        pltpu.make_async_copy(incoming_ref, x_ref, sem.at[0]).wait()
        code_c = code_c_ref[micro]
        code_r = [code_r_ref[micro, at : at + 1, :] for at in range(PER)]
        normed_ref[...] = group_normed(x_ref[...], code_c, code_r, gain_ref[...], bias_ref[...])
        head_r = lax.broadcasted_iota(jnp.int32, (BLOCK, BLOCK), 0) // HD
        head_c = lax.broadcasted_iota(jnp.int32, (BLOCK, BLOCK), 1) // HD
        same = head_r == head_c
        one = same.astype(BF)
        same2 = jnp.concatenate([one, one], axis=0)
        zero = jnp.zeros((BLOCK, BLOCK), BF)
        allowed = []
        for seq in range(PER):
            own = code_c[seq * LEN : (seq + 1) * LEN]
            tile = ((own == code_r[seq]) & (own >= 0)).astype(F32)
            allowed.append(jnp.concatenate([tile] * 4, axis=1))
        dropped = (code_c < 0).astype(F32)

        def head_normed(rows):
            square = dot(jnp.concatenate(parts(rows * rows, 2), axis=1), same2) * (1.0 / HD)
            return (rows * lax.rsqrt(square + 1e-06)).astype(BF)

        normed = normed_ref[...]
        for j in range(6):
            load(j).wait()
            query = head_normed(dot(normed, wq(0, j)))
            key = head_normed(dot(normed, wq(1, j)))
            value = dot(normed, wq(2, j)).astype(BF)
            for seq in range(PER):
                rows = slice(seq * LEN, (seq + 1) * LEN)
                key_bd = jnp.where(same, jnp.concatenate([key[rows]] * 4, axis=0), zero)
                value_bd = jnp.where(same, jnp.concatenate([value[rows]] * 4, axis=0), zero)
                scores = dot_nt(query[rows], key_bd) * (1.0 / math.sqrt(HD))
                expo = jnp.exp(scores) * allowed[seq]
                total = dot(jnp.concatenate(parts(expo, 2), axis=1), same2) + dropped[rows]
                probs = (expo / total).astype(BF)
                attended_ref[rows, j * BLOCK : (j + 1) * BLOCK] = dot(probs, value_bd).astype(BF)
        attended = attended_ref[...]
        for j in range(6):
            load(6 + j).wait()
            for c in (j, j + 6):
                cols = slice(c * BLOCK, (c + 1) * BLOCK)
                y_ref[:, cols] = (x_ref[:, cols].astype(F32) + dot(attended, wo(c))).astype(BF)
        copies = [
            pltpu.make_async_copy(y_ref, out_ref, out_sem.at[0]),
            pltpu.make_async_copy(y_ref, saved_ref.at[micro], out_sem.at[1]),
        ]
        for copy in copies:
            copy.start()
        for copy in copies:
            copy.wait()


def tick(now, at, incoming, tokens, code_c, code_r, gain, bias, weights, saved):
    whole = pl.BlockSpec(memory_space=pltpu.VMEM)
    anywhere = pl.BlockSpec(memory_space=pl.ANY)
    scalar = pl.BlockSpec(memory_space=pltpu.SMEM)
    return pl.pallas_call(
        tick_kernel,
        out_shape=(jax.ShapeDtypeStruct((ROWS, D), BF), jax.ShapeDtypeStruct(saved.shape, BF)),
        in_specs=[scalar, scalar, anywhere, anywhere, whole, whole, whole, whole, anywhere, anywhere],
        out_specs=(anywhere, anywhere),
        scratch_shapes=[
            pltpu.VMEM((ROWS, D), BF),
            pltpu.VMEM((ROWS, D), BF),
            pltpu.VMEM((ROWS, INNER), BF),
            pltpu.VMEM((ROWS, D), BF),
            pltpu.VMEM(weights.shape, BF),
            pltpu.SemaphoreType.DMA((1,)),
            pltpu.SemaphoreType.DMA((12,)),
            pltpu.SemaphoreType.DMA((2,)),
        ],
        input_output_aliases={9: 1},
        compiler_params=pltpu.CompilerParams(vmem_limit_bytes=58 << 20),
    )(now, at, incoming, tokens, code_c, code_r, gain, bias, weights, saved)


def local(tokens, segments, keep_mask, norm_gain, norm_bias, w_qkv, w_out):
    section = lax.axis_index("pipe")
    sections = lax.axis_size("pipe")
    micro = tokens.shape[0] // PER
    qkv, out = w_qkv[0], w_out[0]
    packed = jnp.concatenate(
        [qkv[:, i * INNER : (i + 1) * INNER] for i in range(3)] + [out[:, i * INNER : (i + 1) * INNER] for i in range(2)],
        axis=0,
    )
    weights = lax.all_gather(packed, "dp", axis=0)
    code = jnp.where(keep_mask > 0, segments, -1)
    code_c = code.reshape(micro, ROWS, 1)
    code_r = code.reshape(micro, PER, LEN)
    shaped = tokens.reshape(micro, ROWS, D)
    saved = jnp.zeros(shaped.shape, BF)
    incoming = jnp.zeros((ROWS, D), BF)
    steps = [(i, i + 1) for i in range(sections - 1)]
    at = section.reshape(1)

    def body(now, carried):
        incoming, saved = carried
        result, saved = tick(now.reshape(1), at, incoming, shaped, code_c, code_r, norm_gain, norm_bias, weights, saved)
        return lax.ppermute(result, "pipe", steps), saved

    _, saved = lax.fori_loop(0, micro + sections - 1, body, (incoming, saved))
    return saved.reshape((1,) + tokens.shape)


def solution(mesh):
    placed = (
        P("dp", None, None),
        P("dp", None),
        P("dp", None),
        P("pipe", None),
        P("pipe", None),
        P("pipe", "dp", None),
        P("pipe", "dp", None),
    )
    return jax.shard_map(
        local, mesh=mesh, in_specs=placed, out_specs=P("pipe", "dp", None, None), check_vma=False
    )
```

time: 813 us -> 563 us (0.69)
  matrix products: 148 us -> 0 us
  Pallas kernels: 0 us -> 81.4 us
  waiting for transfers between devices: 506 us -> 446 us
  other arithmetic: 57.7 us -> 0.01 us
  local copies, waits for them, and re-layouts: 63.6 us -> 8.04 us
    dot_general x64 -> x0, matrix products: 148 us -> none  [the longest x8 93.4 us: attend(): projected = jnp.dot(normed, qkv_weight, preferred_element_type=jnp.float32)]
    pallas_call x0 -> x11, Pallas kernels: none -> 81.4 us  [tick(): pl.pallas_call(tick_kernel, out_shape=(jax.ShapeDtypeStruct((ROWS, D), BF...]
    all_gather x2 -> x1, waiting for transfers between devices: 251 us -> 220 us  [local(): weights = lax.all_gather(packed, 'dp', axis=0)]
    ppermute x15 -> x11, waiting for transfers between devices: 254 us -> 225 us  [body(): return (lax.ppermute(result, 'pipe', steps), saved)]
    select_n x15 -> x1, other arithmetic: 15.6 us -> 0.01 us  [local(): code = jnp.where(keep_mask > 0, segments, -1)]
    dynamic_slice x15 -> x0, local copies, waits for them, and re-layouts: 15.4 us -> none  [store(): kept = jnp.where(is_live, result, saved[0, clipped])]
    reduce_sum x40 -> x0, other arithmetic: 13.2 us -> none  [the longest x8 5.05 us: group_normed(): jnp.sum(centred * centred, axis=2)]
    dynamic_update_slice x15 -> x0, other arithmetic: 12.7 us -> none  [store(): return lax.dynamic_update_slice(saved, kept[None, None], (0, clipped, 0, 0))]
  transfers between devices with their start and end apart: 17 -> 12, of which waited for: 17 -> 12; matrix products, arithmetic and copies ran while one was open for 3% -> 0% of each run, Pallas kernels for 0% -> 0%
where the time goes in v1:
time: 563 us
  waiting for transfers between devices  446 us (79%)
  Pallas kernels  81.4 us (14%)
  starting transfers between devices  14.2 us (3%)
  between operations  13.5 us (2%)
  local copies, waits for them, and re-layouts  8.04 us (1%)
    ppermute x11, waiting for transfers between devices, body(): return (lax.ppermute(result, 'pipe', steps), saved)  225 us
    all_gather x1, waiting for transfers between devices, local(): weights = lax.all_gather(packed, 'dp', axis=0)  220 us
    pallas_call x11, Pallas kernels, tick(): pl.pallas_call(tick_kernel, out_shape=(jax.ShapeDtypeStruct((ROWS, D), BF...  81.4 us
    ppermute x11, starting transfers between devices, body(): return (lax.ppermute(result, 'pipe', steps), saved)  14.2 us
  transfers between devices with their start and end apart: 12, of which 12 were waited for; matrix products, arithmetic and copies ran while one was open for 0% of the time, Pallas kernels for 0%

profile of v1, /device:TPU:25, one launch (start us, length us, event | category | flops | bytes accessed | tf_op | source)
XLA Modules:
  0.0 563.0 jit_solution(11526452249667951154)
XLA Ops:
  6.5 1.2 slice_dynamic-update-slice_fusion.2
  8.8 1.1 slice_dynamic-update-slice_fusion
  10.0 1.4 copy-done.1
  11.7 220.4 %all-gather.3.cloned.1.call-done = bf16[12288,1536]{1,0:T(8,128)(2,1)} async-done(((bf16[768,1536]{1,0:T(8,128)(2,1)}), bf16[12288,1536]{1,0:T(8,128)(2,1)}) %all-gather.3.cloned.1.call-update) | async-done | bytes 37748752 | tf_op jit(solution)/shard_map/all_gather | solution.py:211
  233.5 321.1 %while.15 = (s32[]{:T(128)}, bf16[128,3072]{1,0:T(8,128)(2,1)}, bf16[4,128,3072]{2,1,0:T(8,128)(2,1)S(1)}, s32[1]{0:T(128)}, bf16[4,128,3072]{2,1,0:T(8,128)(2,1...) while((s32[]{:T(128)}, bf16[128,3072]{1,0:T(8,128)(2,1)}, ...), condition=%wide.region_1.2_spmd, body=%wide.region_0.1_spmd.sunk | while | flops 2 | bytes 3145877 | solution.py:226
  233.6 1.3 collective-permute-start
  234.9 3.6 collective-permute-done
  238.6 1.3 collective-permute-start
  239.9 12.3 %collective-permute-done = bf16[128,3072]{1,0:T(8,128)(2,1)} collective-permute-done((bf16[128,3072]{1,0:T(8,128)(2,1)}, bf16[128,3072]{1,0:T(8,128)(2,1)}, u32[]{:S(2)}, u32[]{:S(2)}) %collective-permute-start) | collective-permute-done | bytes 786464 | tf_op jit(solution)/shard_map/while/body/eval_jaxpr/ppermute | solution.py:224
  252.4 1.3 collective-permute-start
  253.7 12.3 %collective-permute-done = bf16[128,3072]{1,0:T(8,128)(2,1)} collective-permute-done((bf16[128,3072]{1,0:T(8,128)(2,1)}, bf16[128,3072]{1,0:T(8,128)(2,1)}, u32[]{:S(2)}, u32[]{:S(2)}) %collective-permute-start) | collective-permute-done | bytes 786464 | tf_op jit(solution)/shard_map/while/body/eval_jaxpr/ppermute | solution.py:224
  266.2 1.3 collective-permute-start
  267.5 12.3 %collective-permute-done = bf16[128,3072]{1,0:T(8,128)(2,1)} collective-permute-done((bf16[128,3072]{1,0:T(8,128)(2,1)}, bf16[128,3072]{1,0:T(8,128)(2,1)}, u32[]{:S(2)}, u32[]{:S(2)}) %collective-permute-start) | collective-permute-done | bytes 786464 | tf_op jit(solution)/shard_map/while/body/eval_jaxpr/ppermute | solution.py:224
  280.0 1.3 collective-permute-start
  281.3 12.3 %collective-permute-done = bf16[128,3072]{1,0:T(8,128)(2,1)} collective-permute-done((bf16[128,3072]{1,0:T(8,128)(2,1)}, bf16[128,3072]{1,0:T(8,128)(2,1)}, u32[]{:S(2)}, u32[]{:S(2)}) %collective-permute-start) | collective-permute-done | bytes 786464 | tf_op jit(solution)/shard_map/while/body/eval_jaxpr/ppermute | solution.py:224
  293.7 1.3 collective-permute-start
  295.0 12.3 %collective-permute-done = bf16[128,3072]{1,0:T(8,128)(2,1)} collective-permute-done((bf16[128,3072]{1,0:T(8,128)(2,1)}, bf16[128,3072]{1,0:T(8,128)(2,1)}, u32[]{:S(2)}, u32[]{:S(2)}) %collective-permute-start) | collective-permute-done | bytes 786464 | tf_op jit(solution)/shard_map/while/body/eval_jaxpr/ppermute | solution.py:224
  307.5 1.3 collective-permute-start
  308.8 119.8 %collective-permute-done = bf16[128,3072]{1,0:T(8,128)(2,1)} collective-permute-done((bf16[128,3072]{1,0:T(8,128)(2,1)}, bf16[128,3072]{1,0:T(8,128)(2,1)}, u32[]{:S(2)}, u32[]{:S(2)}) %collective-permute-start) | collective-permute-done | bytes 786464 | tf_op jit(solution)/shard_map/while/body/eval_jaxpr/ppermute | solution.py:224
  428.6 20.1 %eval_jaxpr.5 = (bf16[128,3072]{1,0:T(8,128)(2,1)}, bf16[4,128,3072]{2,1,0:T(8,128)(2,1)S(1)}) custom-call(s32[1]{0:T(128)} %bitcast.9.now_ref, s32[1]{0:T(128)} %get-tuple-element.279.at_ref, bf16[128,3072]{1,0:T(8,128)(2,1)} %get-tuple-element.266.incoming_ref, ...), custom_call_target="tpu_custom_call", output_to_operand_aliasing={{1}: (9, {})} | custom-call | tf_op jit(solution)/shard_map/while/body/eval_jaxpr/pallas_call | solution.py:182
  448.8 1.3 collective-permute-start
  450.1 12.3 %collective-permute-done = bf16[128,3072]{1,0:T(8,128)(2,1)} collective-permute-done((bf16[128,3072]{1,0:T(8,128)(2,1)}, bf16[128,3072]{1,0:T(8,128)(2,1)}, u32[]{:S(2)}, u32[]{:S(2)}) %collective-permute-start) | collective-permute-done | bytes 786464 | tf_op jit(solution)/shard_map/while/body/eval_jaxpr/ppermute | solution.py:224
  462.4 20.1 %eval_jaxpr.5 = (bf16[128,3072]{1,0:T(8,128)(2,1)}, bf16[4,128,3072]{2,1,0:T(8,128)(2,1)S(1)}) custom-call(s32[1]{0:T(128)} %bitcast.9.now_ref, s32[1]{0:T(128)} %get-tuple-element.279.at_ref, bf16[128,3072]{1,0:T(8,128)(2,1)} %get-tuple-element.266.incoming_ref, ...), custom_call_target="tpu_custom_call", output_to_operand_aliasing={{1}: (9, {})} | custom-call | tf_op jit(solution)/shard_map/while/body/eval_jaxpr/pallas_call | solution.py:182
  482.5 1.3 collective-permute-start
  483.8 12.3 %collective-permute-done = bf16[128,3072]{1,0:T(8,128)(2,1)} collective-permute-done((bf16[128,3072]{1,0:T(8,128)(2,1)}, bf16[128,3072]{1,0:T(8,128)(2,1)}, u32[]{:S(2)}, u32[]{:S(2)}) %collective-permute-start) | collective-permute-done | bytes 786464 | tf_op jit(solution)/shard_map/while/body/eval_jaxpr/ppermute | solution.py:224
  496.1 20.1 %eval_jaxpr.5 = (bf16[128,3072]{1,0:T(8,128)(2,1)}, bf16[4,128,3072]{2,1,0:T(8,128)(2,1)S(1)}) custom-call(s32[1]{0:T(128)} %bitcast.9.now_ref, s32[1]{0:T(128)} %get-tuple-element.279.at_ref, bf16[128,3072]{1,0:T(8,128)(2,1)} %get-tuple-element.266.incoming_ref, ...), custom_call_target="tpu_custom_call", output_to_operand_aliasing={{1}: (9, {})} | custom-call | tf_op jit(solution)/shard_map/while/body/eval_jaxpr/pallas_call | solution.py:182
  516.3 1.3 collective-permute-start
  517.6 12.3 %collective-permute-done = bf16[128,3072]{1,0:T(8,128)(2,1)} collective-permute-done((bf16[128,3072]{1,0:T(8,128)(2,1)}, bf16[128,3072]{1,0:T(8,128)(2,1)}, u32[]{:S(2)}, u32[]{:S(2)}) %collective-permute-start) | collective-permute-done | bytes 786464 | tf_op jit(solution)/shard_map/while/body/eval_jaxpr/ppermute | solution.py:224
  529.9 20.1 %eval_jaxpr.5 = (bf16[128,3072]{1,0:T(8,128)(2,1)}, bf16[4,128,3072]{2,1,0:T(8,128)(2,1)S(1)}) custom-call(s32[1]{0:T(128)} %bitcast.9.now_ref, s32[1]{0:T(128)} %get-tuple-element.279.at_ref, bf16[128,3072]{1,0:T(8,128)(2,1)} %get-tuple-element.266.incoming_ref, ...), custom_call_target="tpu_custom_call", output_to_operand_aliasing={{1}: (9, {})} | custom-call | tf_op jit(solution)/shard_map/while/body/eval_jaxpr/pallas_call | solution.py:182
  550.0 1.3 collective-permute-start
  551.3 3.2 collective-permute-done
  554.5 1.7 copy-done
  (28 shorter events, 3.7 us)
Async XLA Ops:
  6.5 3.4 copy-start.2
  6.5 225.6 %all-gather.3.cloned.1.call-start = ((), (), s32[]{:S(2)}) async-start(), calls=%async_computation | async-start | bytes 40108032 | tf_op jit(solution)/shard_map/all_gather | solution.py:211
  8.8 2.7 copy-start.5
  8.8 2.7 copy-start.6
  10.0 1.4 copy-start.1
  11.5 222.0 %copy-start.3 = (f32[1,3072]{1,0:T(1,128)S(1)}, f32[1,3072]{1,0:T(1,128)}, u32[]{:S(2)}) copy-start(f32[1,3072]{1,0:T(1,128)} %param.12) | copy-start | bytes 36868
  11.5 222.0 %copy-start.4 = (f32[1,3072]{1,0:T(1,128)S(1)}, f32[1,3072]{1,0:T(1,128)}, u32[]{:S(2)}) copy-start(f32[1,3072]{1,0:T(1,128)} %param.13) | copy-start | bytes 36868
  233.6 4.9 collective-permute-start
  238.6 13.6 %collective-permute-start = (bf16[128,3072]{1,0:T(8,128)(2,1)}, bf16[128,3072]{1,0:T(8,128)(2,1)}, u32[]{:S(2)}, u32[]{:S(2)}) collective-permute-start(bf16[128,3072]{1,0:T(8,128)(2,1)} %get-tuple-element.252), channel_id=1, source_target_pairs={{0,1},{1,2},{2,3},{3,4},{4,5},{5,6},{6,7},{8,9},{9,10},{10,11},{11... | collective-permute-start | bytes 2359304 | tf_op jit(solution)/shard_map/while/body/eval_jaxpr/ppermute | solution.py:224
  252.4 13.6 %collective-permute-start = (bf16[128,3072]{1,0:T(8,128)(2,1)}, bf16[128,3072]{1,0:T(8,128)(2,1)}, u32[]{:S(2)}, u32[]{:S(2)}) collective-permute-start(bf16[128,3072]{1,0:T(8,128)(2,1)} %get-tuple-element.252), channel_id=1, source_target_pairs={{0,1},{1,2},{2,3},{3,4},{4,5},{5,6},{6,7},{8,9},{9,10},{10,11},{11... | collective-permute-start | bytes 2359304 | tf_op jit(solution)/shard_map/while/body/eval_jaxpr/ppermute | solution.py:224
  266.2 13.6 %collective-permute-start = (bf16[128,3072]{1,0:T(8,128)(2,1)}, bf16[128,3072]{1,0:T(8,128)(2,1)}, u32[]{:S(2)}, u32[]{:S(2)}) collective-permute-start(bf16[128,3072]{1,0:T(8,128)(2,1)} %get-tuple-element.252), channel_id=1, source_target_pairs={{0,1},{1,2},{2,3},{3,4},{4,5},{5,6},{6,7},{8,9},{9,10},{10,11},{11... | collective-permute-start | bytes 2359304 | tf_op jit(solution)/shard_map/while/body/eval_jaxpr/ppermute | solution.py:224
  280.0 13.6 %collective-permute-start = (bf16[128,3072]{1,0:T(8,128)(2,1)}, bf16[128,3072]{1,0:T(8,128)(2,1)}, u32[]{:S(2)}, u32[]{:S(2)}) collective-permute-start(bf16[128,3072]{1,0:T(8,128)(2,1)} %get-tuple-element.252), channel_id=1, source_target_pairs={{0,1},{1,2},{2,3},{3,4},{4,5},{5,6},{6,7},{8,9},{9,10},{10,11},{11... | collective-permute-start | bytes 2359304 | tf_op jit(solution)/shard_map/while/body/eval_jaxpr/ppermute | solution.py:224
  293.7 13.6 %collective-permute-start = (bf16[128,3072]{1,0:T(8,128)(2,1)}, bf16[128,3072]{1,0:T(8,128)(2,1)}, u32[]{:S(2)}, u32[]{:S(2)}) collective-permute-start(bf16[128,3072]{1,0:T(8,128)(2,1)} %get-tuple-element.252), channel_id=1, source_target_pairs={{0,1},{1,2},{2,3},{3,4},{4,5},{5,6},{6,7},{8,9},{9,10},{10,11},{11... | collective-permute-start | bytes 2359304 | tf_op jit(solution)/shard_map/while/body/eval_jaxpr/ppermute | solution.py:224
  307.5 121.1 %collective-permute-start = (bf16[128,3072]{1,0:T(8,128)(2,1)}, bf16[128,3072]{1,0:T(8,128)(2,1)}, u32[]{:S(2)}, u32[]{:S(2)}) collective-permute-start(bf16[128,3072]{1,0:T(8,128)(2,1)} %get-tuple-element.252), channel_id=1, source_target_pairs={{0,1},{1,2},{2,3},{3,4},{4,5},{5,6},{6,7},{8,9},{9,10},{10,11},{11... | collective-permute-start | bytes 2359304 | tf_op jit(solution)/shard_map/while/body/eval_jaxpr/ppermute | solution.py:224
  448.8 13.6 %collective-permute-start = (bf16[128,3072]{1,0:T(8,128)(2,1)}, bf16[128,3072]{1,0:T(8,128)(2,1)}, u32[]{:S(2)}, u32[]{:S(2)}) collective-permute-start(bf16[128,3072]{1,0:T(8,128)(2,1)} %get-tuple-element.252), channel_id=1, source_target_pairs={{0,1},{1,2},{2,3},{3,4},{4,5},{5,6},{6,7},{8,9},{9,10},{10,11},{11... | collective-permute-start | bytes 2359304 | tf_op jit(solution)/shard_map/while/body/eval_jaxpr/ppermute | solution.py:224
  482.5 13.6 %collective-permute-start = (bf16[128,3072]{1,0:T(8,128)(2,1)}, bf16[128,3072]{1,0:T(8,128)(2,1)}, u32[]{:S(2)}, u32[]{:S(2)}) collective-permute-start(bf16[128,3072]{1,0:T(8,128)(2,1)} %get-tuple-element.252), channel_id=1, source_target_pairs={{0,1},{1,2},{2,3},{3,4},{4,5},{5,6},{6,7},{8,9},{9,10},{10,11},{11... | collective-permute-start | bytes 2359304 | tf_op jit(solution)/shard_map/while/body/eval_jaxpr/ppermute | solution.py:224
  516.3 13.6 %collective-permute-start = (bf16[128,3072]{1,0:T(8,128)(2,1)}, bf16[128,3072]{1,0:T(8,128)(2,1)}, u32[]{:S(2)}, u32[]{:S(2)}) collective-permute-start(bf16[128,3072]{1,0:T(8,128)(2,1)} %get-tuple-element.252), channel_id=1, source_target_pairs={{0,1},{1,2},{2,3},{3,4},{4,5},{5,6},{6,7},{8,9},{9,10},{10,11},{11... | collective-permute-start | bytes 2359304 | tf_op jit(solution)/shard_map/while/body/eval_jaxpr/ppermute | solution.py:224
  550.0 4.5 collective-permute-start
  554.5 1.7 copy-start
Sparse Core Ops, SparseCore 0:
  11.6 220.4 all-gather.2

commit v2 on v1

v2 whole, which is shorter than its diff:
```python
import functools
import math

import jax
import jax.numpy as jnp
from jax import lax
from jax.experimental import pallas as pl
from jax.experimental.pallas import tpu as pltpu
from jax.sharding import PartitionSpec as P

D = 3072
HEADS = 24
HD = 64
GROUPS = 32
IMGS = 6
INNER = 1536
WIDTH = D // GROUPS
LEN = 64
PER = 2
ROWS = PER * LEN
BLOCK = 256
BF = jnp.bfloat16
F32 = jnp.float32

norm_eps = 1e-05


def parts(value, count):
    found = []
    for at in range(count):
        piece = value.astype(BF)
        found.append(piece)
        if at + 1 < count:
            value = value - piece.astype(F32)
    return found


def dot(a, b):
    return jnp.dot(a, b, preferred_element_type=F32)


def dot_nt(a, b):
    return lax.dot_general(a, b, (((1,), (1,)), ((), ())), preferred_element_type=F32)


def group_normed(x, code_c, code_r, gain, bias, to_channel):
    kept = code_c >= 0
    together = ((code_c == code_r) & kept).astype(BF)
    counted = jnp.maximum(jnp.sum(together.astype(F32), axis=1, keepdims=True) * WIDTH, 1.0)

    def image_mean(rows):
        sums = dot_nt(rows, to_channel[:GROUPS])
        sums = dot(together, jnp.concatenate(parts(sums, 3), axis=1))
        return (sums[:, :GROUPS] + sums[:, GROUPS : 2 * GROUPS] + sums[:, 2 * GROUPS :]) / counted

    def of_channels(per_group):
        return dot(jnp.concatenate(parts(per_group, 3), axis=1), to_channel)

    centred = x.astype(F32) - of_channels(image_mean(x))
    inverse = lax.rsqrt(image_mean((centred * centred).astype(BF)) + norm_eps)
    return ((centred * of_channels(inverse) * gain + bias) * kept.astype(F32)).astype(BF)


def tick_kernel(now, at_ref, incoming_ref, tokens_ref, code_c_ref, code_r_ref, gain_ref, bias_ref, groups_ref, w_ref, *rest):
    out_ref, saved_ref, x_ref, normed_ref, attended_ref, sem, out_sem = rest[-7:]
    mine = now - at_ref[0]
    micros = tokens_ref.shape[0]
    micro = jnp.clip(mine, 0, micros - 1)

    def wq(part, j):
        return w_ref[:, part * 192 : (part + 1) * 192, j * BLOCK : (j + 1) * BLOCK].reshape(D, BLOCK)

    def wo(c):
        top = 576 + 96 * (c // 6)
        return w_ref[:, top : top + 96, c % 6 * BLOCK : (c % 6 + 1) * BLOCK].reshape(INNER, BLOCK)

    def save(c):
        cols = pl.ds(c * BLOCK, BLOCK)
        return pltpu.make_async_copy(out_ref.at[:, cols], saved_ref.at[micro, :, cols], out_sem.at[c])

    @pl.when((mine >= 0) & (mine < micros))
    def _():
        @pl.when(at_ref[0] == 0)
        def _():
            copy = pltpu.make_async_copy(tokens_ref.at[micro], x_ref, sem.at[0])
            copy.start()
            copy.wait()

        @pl.when(at_ref[0] != 0)
        def _():
            x_ref[...] = incoming_ref[...]

        code_c = code_c_ref[micro]
        code_r = code_r_ref[micro]
        normed_ref[...] = group_normed(x_ref[...], code_c, code_r, gain_ref[...], bias_ref[...], groups_ref[...])
        head_r = lax.broadcasted_iota(jnp.int32, (BLOCK, BLOCK), 0) // HD
        head_c = lax.broadcasted_iota(jnp.int32, (BLOCK, BLOCK), 1) // HD
        same = head_r == head_c
        one = same.astype(BF)
        zero = jnp.zeros((BLOCK, BLOCK), BF)
        allowed = []
        for seq in range(PER):
            own = code_c[seq * LEN : (seq + 1) * LEN]
            tile = ((own == code_r[:, seq * LEN : (seq + 1) * LEN]) & (own >= 0)).astype(F32)
            allowed.append(jnp.concatenate([tile] * 4, axis=1))
        dropped = (code_c < 0).astype(F32)
        normed = normed_ref[...]
        def project(j):
            return dot(normed, wq(0, j)), dot(normed, wq(1, j)), dot(normed, wq(2, j))

        def attend(j, query, key, value):
            pair = jnp.concatenate([query, key], axis=0)
            square = dot((pair * pair).astype(BF), one) * (1.0 / HD)
            pair = pair * lax.rsqrt(square + 1e-06)
            query = (pair[:ROWS] * (1.0 / math.sqrt(HD))).astype(BF)
            key = pair[ROWS:].astype(BF)
            value = value.astype(BF)
            for seq in range(PER):
                rows = slice(seq * LEN, (seq + 1) * LEN)
                key_bd = jnp.where(same, jnp.concatenate([key[rows]] * 4, axis=0), zero)
                value_bd = jnp.where(same, jnp.concatenate([value[rows]] * 4, axis=0), zero)
                expo = (jnp.exp(dot_nt(query[rows], key_bd)) * allowed[seq]).astype(BF)
                both = dot(expo, jnp.concatenate([value_bd, one], axis=1))
                found = both[:, :BLOCK] / (both[:, BLOCK:] + dropped[rows])
                attended_ref[rows, j * BLOCK : (j + 1) * BLOCK] = found.astype(BF)

        ready = project(0)
        for j in range(6):
            following = project(j + 1) if j < 5 else None
            attend(j, *ready)
            ready = following
        attended = attended_ref[...]
        for j in range(6):
            for c in (j, j + 6):
                cols = slice(c * BLOCK, (c + 1) * BLOCK)
                out_ref[:, cols] = (x_ref[:, cols].astype(F32) + dot(attended, wo(c))).astype(BF)
                save(c).start()
        for c in range(12):
            save(c).wait()


def tick(now, at, incoming, tokens, code_c, code_r, gain, bias, groups, weights, saved):
    whole = pl.BlockSpec(memory_space=pltpu.VMEM)
    anywhere = pl.BlockSpec(memory_space=pl.ANY)
    scalar = pl.BlockSpec(memory_space=pltpu.SMEM)
    return pl.pallas_call(
        functools.partial(tick_kernel, now),
        out_shape=(jax.ShapeDtypeStruct((ROWS, D), BF), jax.ShapeDtypeStruct(tokens.shape, BF)),
        in_specs=[scalar, whole, anywhere, whole, whole, whole, whole, whole, whole] + [anywhere] * len(saved),
        out_specs=(whole, anywhere),
        scratch_shapes=[
            pltpu.VMEM((ROWS, D), BF),
            pltpu.VMEM((ROWS, D), BF),
            pltpu.VMEM((ROWS, INNER), BF),
            pltpu.SemaphoreType.DMA((1,)),
            pltpu.SemaphoreType.DMA((12,)),
        ],
        input_output_aliases={9: 1} if saved else {},
        compiler_params=pltpu.CompilerParams(vmem_limit_bytes=18 << 20),
    )(at, incoming, tokens, code_c, code_r, gain, bias, groups, weights, *saved)


def local(tokens, segments, keep_mask, norm_gain, norm_bias, w_qkv, w_out):
    section = lax.axis_index("pipe")
    sections = lax.axis_size("pipe")
    micro = tokens.shape[0] // PER
    qkv, out = w_qkv[0], w_out[0]
    packed = jnp.concatenate(
        [qkv[:, i * INNER : (i + 1) * INNER] for i in range(3)] + [out[:, i * INNER : (i + 1) * INNER] for i in range(2)],
        axis=0,
    )
    weights = lax.all_gather(packed, "dp", axis=0)
    place = lax.broadcasted_iota(jnp.int32, segments.shape, 0) % PER * IMGS
    code = jnp.where(keep_mask > 0, segments + place, -1)
    code_c = code.reshape(micro, ROWS, 1)
    code_r = code.reshape(micro, 1, ROWS)
    owner = lax.broadcasted_iota(jnp.int32, (GROUPS * 3, D), 0) % GROUPS
    groups = (lax.broadcasted_iota(jnp.int32, (GROUPS * 3, D), 1) // WIDTH == owner).astype(BF)
    shaped = tokens.reshape(micro, ROWS, D)
    saved = []
    incoming = shaped[0]
    steps = [(i, i + 1) for i in range(sections - 1)]
    at = section.reshape(1)

    weights = pltpu.with_memory_space_constraint(weights, pltpu.VMEM)
    for now in range(micro + sections - 1):
        result, *saved = tick(now, at, incoming, shaped, code_c, code_r, norm_gain, norm_bias, groups, weights, saved)
        if now < micro + sections - 2:
            result = pltpu.with_memory_space_constraint(result, pltpu.VMEM)
            incoming = pltpu.with_memory_space_constraint(lax.ppermute(result, "pipe", steps), pltpu.VMEM)
    return saved[0].reshape((1,) + tokens.shape)


def solution(mesh):
    placed = (
        P("dp", None, None),
        P("dp", None),
        P("dp", None),
        P("pipe", None),
        P("pipe", None),
        P("pipe", "dp", None),
        P("pipe", "dp", None),
    )
    return jax.shard_map(
        local, mesh=mesh, in_specs=placed, out_specs=P("pipe", "dp", None, None), check_vma=False
    )
```

time: 563 us -> 497 us (0.88); the launches traced: 563 us -> 489 us
  waiting for transfers between devices: 446 us -> 354 us
  local copies, waits for them, and re-layouts: 8.04 us -> 20.2 us
  Pallas kernels: 81.4 us -> 87.1 us
    ppermute x11 -> x10, waiting for transfers between devices: 225 us -> 138 us  [local(): lax.ppermute(result, 'pipe', steps)]
    unnamed x18 -> x14, local copies, waits for them, and re-layouts: 6.5 us -> 16.6 us
    pallas_call x11, Pallas kernels: 81.4 us -> 87.1 us  [tick(): pl.pallas_call(functools.partial(tick_kernel, now), out_shape=(jax.ShapeD...]
    ppermute x11 -> x10, starting transfers between devices: 14.2 us -> 12.9 us  [local(): lax.ppermute(result, 'pipe', steps)]
  transfers between devices with their start and end apart: 12 -> 11, of which waited for: 12 -> 11; matrix products, arithmetic and copies ran while one was open for 0% -> 1% of each run, Pallas kernels for 0% -> 0%
where the time goes in v2:
time: 497 us; the launch traced here: 489 us
  waiting for transfers between devices  354 us (71%)
  Pallas kernels  87.1 us (18%)
  local copies, waits for them, and re-layouts  20.2 us (4%)
  between operations  13.9 us (3%)
  starting transfers between devices  12.9 us (3%)
    all_gather x1, waiting for transfers between devices, local(): weights = lax.all_gather(packed, 'dp', axis=0)  216 us
    ppermute x10, waiting for transfers between devices, local(): lax.ppermute(result, 'pipe', steps)  138 us
    pallas_call x11, Pallas kernels, tick(): pl.pallas_call(functools.partial(tick_kernel, now), out_shape=(jax.ShapeD...  87.1 us
    unnamed x14, local copies, waits for them, and re-layouts  16.6 us
    ppermute x10, starting transfers between devices, local(): lax.ppermute(result, 'pipe', steps)  12.9 us
  transfers between devices with their start and end apart: 11, of which 11 were waited for; matrix products, arithmetic and copies ran while one was open for 1% of the time, Pallas kernels for 0%

profile of v2, /device:TPU:25, one launch (start us, length us, event | category | flops | bytes accessed | tf_op | source)
XLA Modules:
  0.0 489.2 jit_solution(12367114592832633278)
XLA Ops:
  10.0 1.4 copy-done.1
  13.1 2.1 slice.19
  16.2 215.9 %all-gather.3.cloned.1.call-done = bf16[12288,1536]{1,0:T(8,128)(2,1)} async-done(((bf16[768,1536]{1,0:T(8,128)(2,1)}), bf16[12288,1536]{1,0:T(8,128)(2,1)}) %all-gather.3.cloned.1.call-update) | async-done | bytes 37748752 | tf_op jit(solution)/shard_map/all_gather | solution.py:172
  232.1 11.7 %copy-done = bf16[12288,1536]{1,0:T(8,128)(2,1)S(1)} copy-done((bf16[12288,1536]{1,0:T(8,128)(2,1)S(1)}, bf16[12288,1536]{1,0:T(8,128)(2,1)}, u32[]{:S(2)}) %copy-start) | copy-done | bytes 37748760
  243.9 2.4 shard_map.73
  246.3 1.3 collective-permute-start
  247.6 3.4 collective-permute-done.incoming_ref
  251.0 8.8 %shard_map.74 = (bf16[128,3072]{1,0:T(8,128)(2,1)}, bf16[4,128,3072]{2,1,0:T(8,128)(2,1)}) custom-call(s32[1]{0:T(128)} %bitcast.at_ref, bf16[128,3072]{1,0:T(8,128)(2,1)S(1)} %collective-permute-done.incoming_ref, bf16[4,128,3072]{2,1,0:T(8,128)(2,1)} %bitcast.19, s32[4,128,1]{2,1,0:T(8,128)} %reshape.23.code_c_ref, ...), custom_call_target="tpu_custom_call", output_to_operand_aliasing={{1}: (9, {})} | custom-call | tf_op jit(solution)/shard_map/pallas_call | solution.py:146
  259.8 1.3 collective-permute-start.1
  261.1 12.2 %collective-permute-done.1.incoming_ref = bf16[128,3072]{1,0:T(8,128)(2,1)S(1)} collective-permute-done((bf16[128,3072]{1,0:T(8,128)(2,1)}, bf16[128,3072]{1,0:T(8,128)(2,1)S(1)}, u32[]{:S(2)}, u32[]{:S(2)}) %collective-permute-start.1) | collective-permute-done | bytes 786464 | tf_op jit(solution)/shard_map/ppermute | solution.py:190
  273.3 2.2 shard_map.75
  275.5 1.3 collective-permute-start.2
  276.8 12.2 %collective-permute-done.2.incoming_ref = bf16[128,3072]{1,0:T(8,128)(2,1)S(1)} collective-permute-done((bf16[128,3072]{1,0:T(8,128)(2,1)}, bf16[128,3072]{1,0:T(8,128)(2,1)S(1)}, u32[]{:S(2)}, u32[]{:S(2)}) %collective-permute-start.2) | collective-permute-done | bytes 786464 | tf_op jit(solution)/shard_map/ppermute | solution.py:190
  289.1 8.5 %shard_map.76 = (bf16[128,3072]{1,0:T(8,128)(2,1)}, bf16[4,128,3072]{2,1,0:T(8,128)(2,1)}) custom-call(s32[1]{0:T(128)} %bitcast.at_ref, bf16[128,3072]{1,0:T(8,128)(2,1)S(1)} %collective-permute-done.2.incoming_ref, bf16[4,128,3072]{2,1,0:T(8,128)(2,1)} %bitcast.21, s32[4,128,1]{2,1,0:T(8,128)} %reshape.23.code_c_ref, ...), custom_call_target="tpu_custom_call", output_to_operand_aliasing={{1}: (9, {})} | custom-call | tf_op jit(solution)/shard_map/pallas_call | solution.py:146
  297.6 1.3 collective-permute-start.3
  298.9 12.2 %collective-permute-done.3.incoming_ref = bf16[128,3072]{1,0:T(8,128)(2,1)S(1)} collective-permute-done((bf16[128,3072]{1,0:T(8,128)(2,1)}, bf16[128,3072]{1,0:T(8,128)(2,1)S(1)}, u32[]{:S(2)}, u32[]{:S(2)}) %collective-permute-start.3) | collective-permute-done | bytes 786464 | tf_op jit(solution)/shard_map/ppermute | solution.py:190
  311.1 2.2 shard_map.77
  313.3 1.3 collective-permute-start.4
  314.6 12.2 %collective-permute-done.4.incoming_ref = bf16[128,3072]{1,0:T(8,128)(2,1)S(1)} collective-permute-done((bf16[128,3072]{1,0:T(8,128)(2,1)}, bf16[128,3072]{1,0:T(8,128)(2,1)S(1)}, u32[]{:S(2)}, u32[]{:S(2)}) %collective-permute-start.4) | collective-permute-done | bytes 786464 | tf_op jit(solution)/shard_map/ppermute | solution.py:190
  326.9 8.7 %shard_map.78 = (bf16[128,3072]{1,0:T(8,128)(2,1)}, bf16[4,128,3072]{2,1,0:T(8,128)(2,1)}) custom-call(s32[1]{0:T(128)} %bitcast.at_ref, bf16[128,3072]{1,0:T(8,128)(2,1)S(1)} %collective-permute-done.4.incoming_ref, bf16[4,128,3072]{2,1,0:T(8,128)(2,1)} %bitcast.23, s32[4,128,1]{2,1,0:T(8,128)} %reshape.23.code_c_ref, ...), custom_call_target="tpu_custom_call", output_to_operand_aliasing={{1}: (9, {})} | custom-call | tf_op jit(solution)/shard_map/pallas_call | solution.py:146
  335.6 1.3 collective-permute-start.5
  336.9 12.2 %collective-permute-done.5.incoming_ref = bf16[128,3072]{1,0:T(8,128)(2,1)S(1)} collective-permute-done((bf16[128,3072]{1,0:T(8,128)(2,1)}, bf16[128,3072]{1,0:T(8,128)(2,1)S(1)}, u32[]{:S(2)}, u32[]{:S(2)}) %collective-permute-start.5) | collective-permute-done | bytes 786464 | tf_op jit(solution)/shard_map/ppermute | solution.py:190
  349.1 2.2 shard_map.79
  352.6 36.9 %collective-permute-done.6.incoming_ref = bf16[128,3072]{1,0:T(8,128)(2,1)S(1)} collective-permute-done((bf16[128,3072]{1,0:T(8,128)(2,1)}, bf16[128,3072]{1,0:T(8,128)(2,1)S(1)}, u32[]{:S(2)}, u32[]{:S(2)}) %collective-permute-start.6) | collective-permute-done | bytes 786464 | tf_op jit(solution)/shard_map/ppermute | solution.py:190
  389.5 13.2 %shard_map.80 = (bf16[128,3072]{1,0:T(8,128)(2,1)}, bf16[4,128,3072]{2,1,0:T(8,128)(2,1)}) custom-call(s32[1]{0:T(128)} %bitcast.at_ref, bf16[128,3072]{1,0:T(8,128)(2,1)S(1)} %collective-permute-done.6.incoming_ref, bf16[4,128,3072]{2,1,0:T(8,128)(2,1)} %bitcast.25, s32[4,128,1]{2,1,0:T(8,128)} %reshape.23.code_c_ref, ...), custom_call_target="tpu_custom_call", output_to_operand_aliasing={{1}: (9, {})} | custom-call | tf_op jit(solution)/shard_map/pallas_call | solution.py:146
  404.0 12.2 %collective-permute-done.7.incoming_ref = bf16[128,3072]{1,0:T(8,128)(2,1)S(1)} collective-permute-done((bf16[128,3072]{1,0:T(8,128)(2,1)}, bf16[128,3072]{1,0:T(8,128)(2,1)S(1)}, u32[]{:S(2)}, u32[]{:S(2)}) %collective-permute-start.7) | collective-permute-done | bytes 786464 | tf_op jit(solution)/shard_map/ppermute | solution.py:190
  416.2 12.7 %shard_map.81 = (bf16[128,3072]{1,0:T(8,128)(2,1)}, bf16[4,128,3072]{2,1,0:T(8,128)(2,1)}) custom-call(s32[1]{0:T(128)} %bitcast.at_ref, bf16[128,3072]{1,0:T(8,128)(2,1)S(1)} %collective-permute-done.7.incoming_ref, bf16[4,128,3072]{2,1,0:T(8,128)(2,1)} %bitcast.26, s32[4,128,1]{2,1,0:T(8,128)} %reshape.23.code_c_ref, ...), custom_call_target="tpu_custom_call", output_to_operand_aliasing={{1}: (9, {})} | custom-call | tf_op jit(solution)/shard_map/pallas_call | solution.py:146
  429.0 1.3 collective-permute-start.8
  430.3 12.2 %collective-permute-done.8.incoming_ref = bf16[128,3072]{1,0:T(8,128)(2,1)S(1)} collective-permute-done((bf16[128,3072]{1,0:T(8,128)(2,1)}, bf16[128,3072]{1,0:T(8,128)(2,1)S(1)}, u32[]{:S(2)}, u32[]{:S(2)}) %collective-permute-start.8) | collective-permute-done | bytes 786464 | tf_op jit(solution)/shard_map/ppermute | solution.py:190
  442.5 13.4 %shard_map.82 = (bf16[128,3072]{1,0:T(8,128)(2,1)}, bf16[4,128,3072]{2,1,0:T(8,128)(2,1)}) custom-call(s32[1]{0:T(128)} %bitcast.at_ref, bf16[128,3072]{1,0:T(8,128)(2,1)S(1)} %collective-permute-done.8.incoming_ref, bf16[4,128,3072]{2,1,0:T(8,128)(2,1)} %bitcast.27, s32[4,128,1]{2,1,0:T(8,128)} %reshape.23.code_c_ref, ...), custom_call_target="tpu_custom_call", output_to_operand_aliasing={{1}: (9, {})} | custom-call | tf_op jit(solution)/shard_map/pallas_call | solution.py:146
  457.1 12.2 %collective-permute-done.9.incoming_ref = bf16[128,3072]{1,0:T(8,128)(2,1)S(1)} collective-permute-done((bf16[128,3072]{1,0:T(8,128)(2,1)}, bf16[128,3072]{1,0:T(8,128)(2,1)S(1)}, u32[]{:S(2)}, u32[]{:S(2)}) %collective-permute-start.9) | collective-permute-done | bytes 786464 | tf_op jit(solution)/shard_map/ppermute | solution.py:190
  469.4 12.7 %shard_map.83 = (bf16[128,3072]{1,0:T(8,128)(2,1)}, bf16[4,128,3072]{2,1,0:T(8,128)(2,1)}) custom-call(s32[1]{0:T(128)} %bitcast.at_ref, bf16[128,3072]{1,0:T(8,128)(2,1)S(1)} %collective-permute-done.9.incoming_ref, bf16[4,128,3072]{2,1,0:T(8,128)(2,1)} %bitcast.28, s32[4,128,1]{2,1,0:T(8,128)} %reshape.23.code_c_ref, ...), custom_call_target="tpu_custom_call", output_to_operand_aliasing={{1}: (9, {})} | custom-call | tf_op jit(solution)/shard_map/pallas_call | solution.py:146
  (28 shorter events, 10.0 us)
Async XLA Ops:
  6.5 3.4 copy-start.2
  6.5 225.6 %all-gather.3.cloned.1.call-start = ((), (), s32[]{:S(2)}) async-start(), calls=%async_computation | async-start | bytes 40108032 | tf_op jit(solution)/shard_map/all_gather | solution.py:172
  8.8 2.7 copy-start.3
  8.8 2.7 copy-start.4
  10.0 1.4 copy-start.1
  232.1 11.7 %copy-start = (bf16[12288,1536]{1,0:T(8,128)(2,1)S(1)}, bf16[12288,1536]{1,0:T(8,128)(2,1)}, u32[]{:S(2)}) copy-start(bf16[12288,1536]{1,0:T(8,128)(2,1)} %all-gather.3.cloned.1.call-done) | copy-start | bytes 113246208
  246.3 4.7 collective-permute-start
  259.8 13.5 %collective-permute-start.1 = (bf16[128,3072]{1,0:T(8,128)(2,1)}, bf16[128,3072]{1,0:T(8,128)(2,1)S(1)}, u32[]{:S(2)}, u32[]{:S(2)}) collective-permute-start(bf16[128,3072]{1,0:T(8,128)(2,1)} %get-tuple-element.28), channel_id=1, source_target_pairs={{0,1},{1,2},{2,3},{3,4},{4,5},{5,6},{6,7},{8,9},{9,10},{10,11},{11... | collective-permute-start | bytes 2359304 | tf_op jit(solution)/shard_map/ppermute | solution.py:190
  275.5 13.5 %collective-permute-start.2 = (bf16[128,3072]{1,0:T(8,128)(2,1)}, bf16[128,3072]{1,0:T(8,128)(2,1)S(1)}, u32[]{:S(2)}, u32[]{:S(2)}) collective-permute-start(bf16[128,3072]{1,0:T(8,128)(2,1)} %get-tuple-element.30), channel_id=1, source_target_pairs={{0,1},{1,2},{2,3},{3,4},{4,5},{5,6},{6,7},{8,9},{9,10},{10,11},{11... | collective-permute-start | bytes 2359304 | tf_op jit(solution)/shard_map/ppermute | solution.py:190
  297.6 13.5 %collective-permute-start.3 = (bf16[128,3072]{1,0:T(8,128)(2,1)}, bf16[128,3072]{1,0:T(8,128)(2,1)S(1)}, u32[]{:S(2)}, u32[]{:S(2)}) collective-permute-start(bf16[128,3072]{1,0:T(8,128)(2,1)} %get-tuple-element.32), channel_id=1, source_target_pairs={{0,1},{1,2},{2,3},{3,4},{4,5},{5,6},{6,7},{8,9},{9,10},{10,11},{11... | collective-permute-start | bytes 2359304 | tf_op jit(solution)/shard_map/ppermute | solution.py:190
  313.3 13.5 %collective-permute-start.4 = (bf16[128,3072]{1,0:T(8,128)(2,1)}, bf16[128,3072]{1,0:T(8,128)(2,1)S(1)}, u32[]{:S(2)}, u32[]{:S(2)}) collective-permute-start(bf16[128,3072]{1,0:T(8,128)(2,1)} %get-tuple-element.34), channel_id=1, source_target_pairs={{0,1},{1,2},{2,3},{3,4},{4,5},{5,6},{6,7},{8,9},{9,10},{10,11},{11... | collective-permute-start | bytes 2359304 | tf_op jit(solution)/shard_map/ppermute | solution.py:190
  335.6 13.5 %collective-permute-start.5 = (bf16[128,3072]{1,0:T(8,128)(2,1)}, bf16[128,3072]{1,0:T(8,128)(2,1)S(1)}, u32[]{:S(2)}, u32[]{:S(2)}) collective-permute-start(bf16[128,3072]{1,0:T(8,128)(2,1)} %get-tuple-element.36), channel_id=1, source_target_pairs={{0,1},{1,2},{2,3},{3,4},{4,5},{5,6},{6,7},{8,9},{9,10},{10,11},{11... | collective-permute-start | bytes 2359304 | tf_op jit(solution)/shard_map/ppermute | solution.py:190
  351.3 38.2 %collective-permute-start.6 = (bf16[128,3072]{1,0:T(8,128)(2,1)}, bf16[128,3072]{1,0:T(8,128)(2,1)S(1)}, u32[]{:S(2)}, u32[]{:S(2)}) collective-permute-start(bf16[128,3072]{1,0:T(8,128)(2,1)} %get-tuple-element.38), channel_id=1, source_target_pairs={{0,1},{1,2},{2,3},{3,4},{4,5},{5,6},{6,7},{8,9},{9,10},{10,11},{11... | collective-permute-start | bytes 2359304 | tf_op jit(solution)/shard_map/ppermute | solution.py:190
  402.7 13.5 %collective-permute-start.7 = (bf16[128,3072]{1,0:T(8,128)(2,1)}, bf16[128,3072]{1,0:T(8,128)(2,1)S(1)}, u32[]{:S(2)}, u32[]{:S(2)}) collective-permute-start(bf16[128,3072]{1,0:T(8,128)(2,1)} %get-tuple-element.40), channel_id=1, source_target_pairs={{0,1},{1,2},{2,3},{3,4},{4,5},{5,6},{6,7},{8,9},{9,10},{10,11},{11... | collective-permute-start | bytes 2359304 | tf_op jit(solution)/shard_map/ppermute | solution.py:190
  429.0 13.5 %collective-permute-start.8 = (bf16[128,3072]{1,0:T(8,128)(2,1)}, bf16[128,3072]{1,0:T(8,128)(2,1)S(1)}, u32[]{:S(2)}, u32[]{:S(2)}) collective-permute-start(bf16[128,3072]{1,0:T(8,128)(2,1)} %get-tuple-element.42), channel_id=1, source_target_pairs={{0,1},{1,2},{2,3},{3,4},{4,5},{5,6},{6,7},{8,9},{9,10},{10,11},{11... | collective-permute-start | bytes 2359304 | tf_op jit(solution)/shard_map/ppermute | solution.py:190
  455.8 13.5 %collective-permute-start.9 = (bf16[128,3072]{1,0:T(8,128)(2,1)}, bf16[128,3072]{1,0:T(8,128)(2,1)S(1)}, u32[]{:S(2)}, u32[]{:S(2)}) collective-permute-start(bf16[128,3072]{1,0:T(8,128)(2,1)} %get-tuple-element.44), channel_id=1, source_target_pairs={{0,1},{1,2},{2,3},{3,4},{4,5},{5,6},{6,7},{8,9},{9,10},{10,11},{11... | collective-permute-start | bytes 2359304 | tf_op jit(solution)/shard_map/ppermute | solution.py:190
Sparse Core Ops, SparseCore 0:
  11.6 220.4 all-gather.2
